TPU v7x, 32 devices: a whole 2x2x4 slice. The times are simulated.
32 devices in a mesh: fsdp: 8 (over z, core), seq: 4 (over y, x).
Axes of the slice: x: 2, y: 2, z: 4, core: 2. Of those that a mesh axis runs over, the one named last changes fastest.
Arguments:
- inputs: bfloat16 [8, 1024, 2048], P('fsdp', 'seq'), may hold values from -6 to 6
- cotangent: bfloat16 [8, 1024, 2048], P('fsdp', 'seq'), may hold values from -6 to 6
- norm1_gain: bfloat16 [2048], P('fsdp'), may hold values from 0.5 to 1.5
- w_qkv: bfloat16 [2048, 6144], P('fsdp'), may hold values from -0.125 to 0.125
- w_beta: bfloat16 [2048, 16], P('fsdp'), may hold values from -0.125 to 0.125
- conv_weight: bfloat16 [2048, 12], P('fsdp'), may hold values from -3 to 3
- out_gain: bfloat16 [128], replicated, may hold values from 0.5 to 1.5
- w_out: bfloat16 [2048, 2048], P('fsdp'), may hold values from -0.125 to 0.125
- norm2_gain: bfloat16 [2048], P('fsdp'), may hold values from 0.5 to 1.5
- w_gate_up: bfloat16 [2048, 11264], P('fsdp'), may hold values from -0.125 to 0.125
- w_down: bfloat16 [5632, 2048], P('fsdp'), may hold values from -0.15625 to 0.15625
Outputs:
- output: bfloat16 [8, 1024, 2048], P('fsdp', 'seq')
- grad_input: float32 [8, 1024, 2048], P('fsdp', 'seq')
- grad_norm1_gain: float32 [2048], P('fsdp')
- grad_w_qkv: float32 [2048, 6144], P('fsdp')
- grad_w_beta: float32 [2048, 16], P('fsdp')
- grad_conv_weight: float32 [2048, 12], P('fsdp')
- grad_out_gain: float32 [128], replicated
- grad_w_out: float32 [2048, 2048], P('fsdp')
- grad_norm2_gain: float32 [2048], P('fsdp')
- grad_w_gate_up: float32 [2048, 11264], P('fsdp')
- grad_w_down: float32 [5632, 2048], P('fsdp')
All inputs are finite; a program needn't handle non-finite values.
Results may differ from a plain program's by a relative error of at most 0.023.
Values may be sent and summed in bfloat16 or wider, within the bound.
A program may use at most 448 MiB of HBM per device.

v0:
```python
import jax
import jax.numpy as jnp
from jax import lax
from jax.sharding import PartitionSpec as P

H = 16
DK = 128
SPAN = 64
EPS = 1e-06
HIGH = lax.Precision.HIGHEST


def from_behind(array, axis, by):
    devices = lax.axis_size(axis)
    pairs = [(i, i + by) for i in range(devices) if 0 <= i + by < devices]
    return lax.ppermute(array, axis, pairs)


def rms_scale(values, gain):
    return values * lax.rsqrt(jnp.mean(values * values, axis=-1, keepdims=True) + EPS) * gain


def conv_table(conv_full):
    width = conv_full.shape[0]
    tap_count = conv_full.shape[1] // 3
    return (
        conv_full.astype(jnp.float32)
        .reshape(width, 3, tap_count)
        .transpose(1, 0, 2)
        .reshape(3 * width, tap_count)
    )


def pre_mix(extended, table, beta_logits):
    tap_count = table.shape[1]
    length = extended.shape[1] - tap_count + 1
    sequences = extended.shape[0]
    width = extended.shape[2] // 3
    mixed = extended[:, 0:length, :] * table[:, 0]
    for tap_index in range(1, tap_count):
        mixed = mixed + extended[:, tap_index : tap_index + length, :] * table[:, tap_index]
    active = jax.nn.silu(mixed)
    query = active[:, :, :width].reshape(sequences, length, H, DK) * DK ** (-0.5)
    key = active[:, :, width : 2 * width].reshape(sequences, length, H, DK)
    key = key * lax.rsqrt(jnp.sum(key * key, axis=-1, keepdims=True) + EPS)
    value = active[:, :, 2 * width :].reshape(sequences, length, H, DK)
    return (query, key, value, jax.nn.sigmoid(beta_logits))


def delta_rule(query, key, value, beta):
    sequences, length, heads, depth = query.shape
    count = length // SPAN

    def blocks(array):
        return array.reshape(sequences, count, SPAN, heads, -1).transpose(1, 0, 3, 2, 4)

    q_blocks = blocks(query)
    k_blocks = blocks(key)
    v_blocks = blocks(value)
    b_blocks = blocks(beta[..., None])
    gram = jnp.einsum("nshcd,nshmd->nshcm", k_blocks, k_blocks, precision=HIGH)
    below = jnp.tril(jnp.ones((SPAN, SPAN), jnp.float32), -1)
    inclusive = jnp.tril(jnp.ones((SPAN, SPAN), jnp.float32))
    system = jnp.eye(SPAN, dtype=jnp.float32) + below * (b_blocks * gram)
    targets = jnp.concatenate([b_blocks * k_blocks, b_blocks * v_blocks], axis=-1)
    solved = lax.linalg.triangular_solve(
        system, targets, left_side=True, lower=True, unit_diagonal=True
    )
    wy_key = solved[..., :depth]
    wy_value = solved[..., depth:]
    within = inclusive * jnp.einsum("nshcd,nshmd->nshcm", q_blocks, k_blocks, precision=HIGH)

    def advance(state, pieces):
        key_part, value_part, query_part, key_raw, attend = pieces
        fresh = value_part - jnp.einsum("shcd,shde->shce", key_part, state, precision=HIGH)
        result = jnp.einsum("shcd,shde->shce", query_part, state, precision=HIGH)
        result = result + jnp.einsum("shcm,shme->shce", attend, fresh, precision=HIGH)
        state = state + jnp.einsum("shcd,shce->shde", key_raw, fresh, precision=HIGH)
        return (state, result)

    start = jnp.zeros((sequences, heads, depth, value.shape[-1]), jnp.float32)
    final, outputs = lax.scan(advance, start, (wy_key, wy_value, q_blocks, k_blocks, within))
    return outputs.transpose(1, 0, 3, 2, 4).reshape(sequences, length, heads, -1)


def row_term(left, right):

    def term(start, count):
        return lax.dot_general(
            left, right, (((0,), (0,)), ((), ())), preferred_element_type=jnp.float32
        )

    return term


def reduce_rows(term, total_rows):
    shards = lax.axis_size("fsdp")
    summed = lax.psum_scatter(
        term(jnp.int32(0), total_rows // shards * lax.axis_size("fsdp")).astype(jnp.bfloat16),
        "fsdp",
        scatter_dimension=0,
        tiled=True,
    )
    return lax.psum(summed, "seq").astype(jnp.float32)


def against(left, right):
    return lax.dot_general(
        left, right, (((1,), (1,)), ((), ())), preferred_element_type=jnp.float32
    )


def per_device(
    inputs,
    cotangent,
    norm1_gain,
    w_qkv,
    w_beta,
    conv_weight,
    out_gain,
    w_out,
    norm2_gain,
    w_gate_up,
    w_down,
):
    gathered = (
        lax.all_gather(norm1_gain, "fsdp", axis=0, tiled=True),
        lax.all_gather(w_qkv, "fsdp", axis=0, tiled=True),
        lax.all_gather(w_beta, "fsdp", axis=0, tiled=True),
        lax.all_gather(conv_weight, "fsdp", axis=0, tiled=True),
        lax.all_gather(w_out, "fsdp", axis=0, tiled=True),
        lax.all_gather(norm2_gain, "fsdp", axis=0, tiled=True),
        lax.all_gather(w_gate_up, "fsdp", axis=0, tiled=True),
    )
    gain_first, qkv_full, beta_full, conv_full, out_full, gain_second, gate_up_full = gathered
    down_full = lax.all_gather(w_down, "fsdp", axis=0, tiled=True)
    sequences, block, width = inputs.shape
    tokens = sequences * block
    hidden_width = down_full.shape[0]
    edge_rows = conv_full.shape[1] // 3 - 1
    residual = inputs.astype(jnp.float32).reshape(tokens, width)
    first_normed, first_back = jax.vjp(rms_scale, residual, gain_first.astype(jnp.float32))
    normed_first = first_normed.astype(jnp.bfloat16)
    projected = jnp.dot(normed_first, qkv_full, preferred_element_type=jnp.float32)
    projected = projected.astype(jnp.bfloat16).reshape(sequences, block, 3 * width)
    beta_logits = jnp.dot(normed_first, beta_full, preferred_element_type=jnp.float32).reshape(
        sequences, block, -1
    )
    before = from_behind(projected[:, block - edge_rows :, :], "seq", 1)
    extended = jnp.concatenate([before, projected], axis=1).astype(jnp.float32)
    table = conv_table(conv_full)
    mixer_inputs, mixer_back = jax.vjp(pre_mix, extended, table, beta_logits)
    sent_query = mixer_inputs[0].astype(jnp.bfloat16)
    sent_key = mixer_inputs[1].astype(jnp.bfloat16)
    sent_value = mixer_inputs[2].astype(jnp.bfloat16)
    sent_beta = mixer_inputs[3].astype(jnp.bfloat16)
    query, key, value, beta = (
        lax.all_to_all(sent_query, "seq", split_axis=2, concat_axis=1, tiled=True),
        lax.all_to_all(sent_key, "seq", split_axis=2, concat_axis=1, tiled=True),
        lax.all_to_all(sent_value, "seq", split_axis=2, concat_axis=1, tiled=True),
        lax.all_to_all(sent_beta, "seq", split_axis=2, concat_axis=1, tiled=True),
    )
    heads_out, delta_back = jax.vjp(
        delta_rule,
        query.astype(jnp.float32),
        key.astype(jnp.float32),
        value.astype(jnp.float32),
        beta.astype(jnp.float32),
    )
    returned = lax.all_to_all(
        heads_out.astype(jnp.bfloat16), "seq", split_axis=1, concat_axis=2, tiled=True
    )
    normed_heads, heads_back = jax.vjp(
        rms_scale, returned.astype(jnp.float32), out_gain.astype(jnp.float32)
    )
    attn_in = normed_heads.astype(jnp.bfloat16).reshape(tokens, width)
    middle = residual + jnp.dot(attn_in, out_full, preferred_element_type=jnp.float32)
    second_normed, second_back = jax.vjp(rms_scale, middle, gain_second.astype(jnp.float32))
    ffn_in = second_normed.astype(jnp.bfloat16)
    gate_up = jnp.dot(ffn_in, gate_up_full, preferred_element_type=jnp.float32)
    gate = gate_up[:, :hidden_width]
    upward = gate_up[:, hidden_width:]
    sigma = jax.nn.sigmoid(gate)
    hidden = (gate * sigma * upward).astype(jnp.bfloat16)
    result = middle + jnp.dot(hidden, down_full, preferred_element_type=jnp.float32)
    output = result.astype(jnp.bfloat16).reshape(sequences, block, width)
    upstream = cotangent.reshape(tokens, width)
    grad_down = reduce_rows(row_term(hidden, upstream), hidden_width)
    grad_hidden = against(upstream, down_full)
    grad_gate = grad_hidden * upward * sigma * (1.0 + gate * (1.0 - sigma))
    grad_up = grad_hidden * gate * sigma
    grad_gate_up = jnp.concatenate([grad_gate, grad_up], axis=1).astype(jnp.bfloat16)
    grad_w_gate_up = reduce_rows(row_term(ffn_in, grad_gate_up), width)
    grad_ffn_in = against(grad_gate_up, gate_up_full)
    grad_middle_norm, grad_gain_second = second_back(grad_ffn_in)
    grad_middle = upstream.astype(jnp.float32) + grad_middle_norm
    grad_branch = grad_middle.astype(jnp.bfloat16)
    grad_w_out = reduce_rows(row_term(attn_in, grad_branch), width)
    grad_attn_in = against(grad_branch, out_full).reshape(sequences, block, H, DK)
    grad_returned, grad_gain_heads = heads_back(grad_attn_in)
    grad_heads = lax.all_to_all(
        grad_returned.astype(jnp.bfloat16), "seq", split_axis=2, concat_axis=1, tiled=True
    )
    grad_query, grad_key, grad_value, grad_beta = delta_back(grad_heads.astype(jnp.float32))
    back_query, back_key, back_value, back_beta = (
        lax.all_to_all(
            grad_query.astype(jnp.bfloat16), "seq", split_axis=1, concat_axis=2, tiled=True
        ),
        lax.all_to_all(
            grad_key.astype(jnp.bfloat16), "seq", split_axis=1, concat_axis=2, tiled=True
        ),
        lax.all_to_all(
            grad_value.astype(jnp.bfloat16), "seq", split_axis=1, concat_axis=2, tiled=True
        ),
        lax.all_to_all(
            grad_beta.astype(jnp.bfloat16), "seq", split_axis=1, concat_axis=2, tiled=True
        ),
    )
    grad_extended, grad_table, grad_logits = mixer_back(
        (
            back_query.astype(jnp.float32),
            back_key.astype(jnp.float32),
            back_value.astype(jnp.float32),
            back_beta.astype(jnp.float32),
        )
    )
    after = from_behind(grad_extended[:, :edge_rows, :].astype(jnp.bfloat16), "seq", -1).astype(
        jnp.float32
    )
    grad_projected = grad_extended[:, edge_rows:, :]
    grad_projected = grad_projected.at[:, block - edge_rows :, :].add(after)
    grad_proj_low = grad_projected.astype(jnp.bfloat16).reshape(tokens, 3 * width)
    grad_logits_low = grad_logits.astype(jnp.bfloat16).reshape(tokens, -1)
    grad_w_qkv = reduce_rows(row_term(normed_first, grad_proj_low), width)
    grad_beta_full = lax.dot_general(
        normed_first, grad_logits_low, (((0,), (0,)), ((), ())), preferred_element_type=jnp.float32
    )
    grad_normed_first = against(grad_proj_low, qkv_full) + against(grad_logits_low, beta_full)
    grad_residual_norm, grad_gain_first = first_back(grad_normed_first)
    grad_input = (grad_middle + grad_residual_norm).reshape(sequences, block, width)
    grad_conv = grad_table.reshape(3, width, -1).transpose(1, 0, 2).reshape(width, -1)
    summed = lax.psum(
        (grad_gain_first, grad_beta_full, grad_conv, grad_gain_heads, grad_gain_second),
        ("fsdp", "seq"),
    )
    share = width // lax.axis_size("fsdp")
    offset = lax.axis_index("fsdp") * share

    def own_rows(array):
        return lax.dynamic_slice_in_dim(array, offset, share, 0)

    return (
        output,
        grad_input,
        own_rows(summed[0]),
        grad_w_qkv,
        own_rows(summed[1]),
        own_rows(summed[2]),
        summed[3],
        grad_w_out,
        own_rows(summed[4]),
        grad_w_gate_up,
        grad_down,
    )


def solution(mesh):
    in_specs = (
        P("fsdp", "seq", None),
        P("fsdp", "seq", None),
        P("fsdp"),
        P("fsdp", None),
        P("fsdp", None),
        P("fsdp", None),
        P(),
        P("fsdp", None),
        P("fsdp"),
        P("fsdp", None),
        P("fsdp", None),
    )
    out_specs = (
        P("fsdp", "seq", None),
        P("fsdp", "seq", None),
        P("fsdp"),
        P("fsdp", None),
        P("fsdp", None),
        P("fsdp", None),
        P(),
        P("fsdp", None),
        P("fsdp"),
        P("fsdp", None),
        P("fsdp", None),
    )
    return jax.shard_map(
        per_device, mesh=mesh, in_specs=in_specs, out_specs=out_specs, check_vma=False
    )
```

profile of v0, /device:TPU:0, one launch (start us, length us, event | category | flops | bytes accessed | tf_op | source)
XLA Modules:
  0.0 2502.2 jit_solution(38190960428922679)
XLA Ops:
  10.1 13.6 all-gather
  23.7 24.1 all_gather.27
  54.7 25.3 %all_gather.26 = bf16[2048,12]{0,1:T(8,128)(2,1)S(1)} all-gather(bf16[256,12]{0,1:T(8,128)(2,1)S(1)} %copy-done.77), channel_id=1, replica_groups=mesh['fsdp'=8,'seq'=4] {'fsdp'}, dimensions={0}, use_global_device_ids=true | all-gather | bytes 55296 | tf_op jit(solution)/shard_map/all_gather | solution.py:130
  80.0 153.2 %all-gather.7.cloned.1.call-done = bf16[2048,6144]{1,0:T(8,128)(2,1)} async-done(((bf16[256,6144]{1,0:T(8,128)(2,1)}), bf16[2048,6144]{1,0:T(8,128)(2,1)}) %all-gather.7.cloned.1.call-update) | async-done | bytes 25165840 | tf_op jit(solution)/shard_map/all_gather | solution.py:128
  233.2 12.3 fusion.79
  268.5 12.8 all-to-all-done
  322.4 315.2 %custom-call.7 = f32[16,1,4,1,64,64]{4,5,3,2,1,0:T(8,128)S(1)} custom-call(f32[16,1,4,1,64,64]{5,4,3,2,1,0:T(8,128)} %add_bitcast_fusion), custom_call_target="InvertDiagBlocksLowerTriangular" | custom-call | tf_op jit(solution)/shard_map/jvp()/triangular_solve | solution.py:66
  653.0 107.2 %while.43 = (s32[]{:T(128)}, f32[1,4,128,128]{3,2,1,0:T(8,128)S(1)}, bf16[16,1,4,64,128]{4,3,0,2,1:T(8,128)(2,1)}, f32[16,1,4,128,128]{4,3,2,1,0:T(8,128)}, f32[...) while((s32[]{:T(128)}, ...), condition=%wide.region_3.4_spmd.clone, body=%wide.region_2.3_spmd.clone.sunk | while | flops 176553984 | bytes 3148948 | solution.py:82
  803.1 24.2 fusion.211
  827.3 83.8 %all-gather.13.cloned.1.call-done = bf16[5632,2048]{1,0:T(8,128)(2,1)} async-done(((bf16[704,2048]{1,0:T(8,128)(2,1)}), bf16[5632,2048]{1,0:T(8,128)(2,1)}) %all-gather.13.cloned.1.call-update) | async-done | bytes 23068688 | tf_op jit(solution)/shard_map/all_gather | solution.py:136
  911.2 18.7 multiply_convert_fusion.1
  929.9 22.1 multiply_reduce_fusion.4
  961.1 12.9 convolution_convert_fusion.1
  1002.1 14.2 all-to-all-done.5
  1025.9 241.0 %while.44 = (s32[]{:T(128)}, f32[1,4,128,128]{2,3,1,0:T(8,128)S(1)}, f32[16,1,4,64,128]{4,3,2,1,0:T(8,128)}, f32[16,1,4,64,128]{4,3,2,1,0:T(8,128)}, f32[16,1,4,...) while((s32[]{:T(128)}, ...), condition=%wide.region_9.10_spmd.clone, body=%wide.region_8.9_spmd.clone.sunk | while | flops 352747520 | bytes 4728510 | solution.py:82
  1393.8 14.0 convolution_convert_fusion.2
  1409.4 21.2 convolution_convert_fusion
  1450.2 204.2 %reduce-scatter.7.cloned.1.call-done = bf16[256,6144]{1,0:T(8,128)(2,1)} async-done(((bf16[2048,6144]{1,0:T(8,128)(2,1)}), bf16[256,6144]{1,0:T(8,128)(2,1)}) %reduce-scatter.7.cloned.1.call-update) | async-done | bytes 3145744 | tf_op jit(solution)/shard_map/reduce_scatter | solution.py:98
  1654.4 444.5 %reduce-scatter.13.cloned.1.call-done = bf16[256,11264]{1,0:T(8,128)(2,1)} async-done(((bf16[2048,11264]{1,0:T(8,128)(2,1)}), bf16[256,11264]{1,0:T(8,128)(2,1)}) %reduce-scatter.13.cloned.1.call-update) | async-done | bytes 5767184
  2099.6 12.6 fusion.105
  2114.0 14.4 fusion.110
  2128.4 38.2 %all-reduce.14 = (f32[2048]{0:T(1024)S(1)}, f32[128]{0:T(128)}, f32[2048]{0:T(1024)S(1)}) all-reduce(f32[2048]{0:T(1024)S(1)} %get-tuple-element.617, f32[128]{0:T(128)S(1)} %bitcast_reduce_fusion, f32[2048]{0:T(1024)S(1)} %copy-done.78), channel_id=1, replica_groups=mesh['fsdp'=8,'seq'=4] {'fsdp','seq'}, use_global_device_ids=true, to_apply=%region_16.17 | all-reduce | flops 4224 | bytes 33792 | tf_op jit(solution)/shard_map/psum | solution.py:242
  2171.4 58.3 %all-reduce.20.cloned.1.call-done = (f32[2048,16]{0,1:T(8,128)}, f32[2048,12]{0,1:T(8,128)}) async-done(((f32[2048,16]{0,1:T(8,128)}, f32[2048,12]{0,1:T(8,128)}), (f32[2048,16]{0,1:T(8,128)}, f32[2048,12]{0,1:T(8,128)})) %all-reduce.20.cloned.1.call-update) | async-done | bytes 229392 | tf_op jit(solution)/shard_map/psum | solution.py:242
  2232.4 246.7 %all-reduce.22.cloned.1.call-done = (bf16[256,6144]{1,0:T(8,128)(2,1)}, bf16[256,2048]{1,0:T(8,128)(2,1)}, bf16[256,11264]{1,0:T(8,128)(2,1)}, bf16[704,2048]{1,0:T(8,128)(2,1)}) async-done(((bf16[256,6144]{1,0:T(8,128)(2,1)}, bf16[256,2048]{1,0:T(8,128)(2,1)}, bf16[256,11264]{1,0:T(8,128)(2,1)}, bf16[704,2048]{1,0:T(8,128)(2,1)}), (bf16[256,6144]{1,0:T(8,128)(2,1)}, bf16[256,2048]{1,0:T(8,128)(2,1)}, ...) | async-done | bytes 12845072 | tf_op jit(solution)/shard_map/psum | solution.py:104
  (580 shorter events, 698.9 us)
Async XLA Ops:
  7.2 226.0 %all-gather.7.cloned.1.call-start = ((), (), s32[]{:S(2)}) async-start(), calls=%async_computation.14 | async-start | bytes 28311552 | tf_op jit(solution)/shard_map/all_gather | solution.py:128
  7.9 788.6 %all-gather.9.cloned.1.call-start = ((), (), s32[]{:S(2)}) async-start(), calls=%async_computation.15 | async-start | bytes 9437184 | tf_op jit(solution)/shard_map/all_gather | solution.py:131
  8.7 794.4 %all-gather.11.cloned.1.call-start = ((), (), s32[]{:S(2)}) async-start(), calls=%async_computation.16 | async-start | bytes 51904512 | tf_op jit(solution)/shard_map/all_gather | solution.py:133
  9.4 901.7 %all-gather.13.cloned.1.call-start = ((), (), s32[]{:S(2)}) async-start(), calls=%async_computation.17 | async-start | bytes 25952256 | tf_op jit(solution)/shard_map/all_gather | solution.py:136
  23.7 221.9 %copy-start.46 = (f32[8,1,256]{2,1,0:T(1,128)}, f32[8,1,256]{2,1,0:T(1,128)S(1)}, u32[]{:S(2)}) copy-start(f32[8,1,256]{2,1,0:T(1,128)S(1)} %convert_element_type.540) | copy-start | bytes 24580
  51.0 211.7 %all-to-all-start.1 = ((bf16[4,2,512]{2,1,0:T(2,128)(2,1)}), bf16[4,2,512]{2,1,0:T(2,128)(2,1)S(1)}, u32[]{:S(2)}, u32[]{:S(2)}) async-start(bf16[4,2,512]{2,1,0:T(2,128)(2,1)} %reshape.1133), calls=%async_computation.1 | async-start | bytes 16384 | tf_op jit(solution)/shard_map/all_to_all | solution.py:161
  245.6 5.0 collective-permute-start
  262.7 18.6 all-to-all-start
  281.3 17.5 all-to-all-start.3
  299.8 17.3 all-to-all-start.2
  303.8 333.9 %copy-start.44 = (f32[64,64]{1,0:T(8,128)}, f32[64,64]{1,0:T(8,128)S(1)}, u32[]{:S(2)}) copy-start(f32[64,64]{1,0:T(8,128)S(1)} %fusion.200) | copy-start | bytes 49156
  764.0 17.3 all-to-all-start.4
  768.3 681.9 %reduce-scatter.9.cloned.1.call-start = ((), (), s32[]{:S(2)}) async-start(), calls=%async_computation.19 | async-start | bytes 9437184 | tf_op jit(solution)/shard_map/reduce_scatter | solution.py:98
  961.1 489.1 %reduce-scatter.11.cloned.1.call-start = ((), (), s32[]{:S(2)}) async-start(), calls=%async_computation.20 | async-start | bytes 25952256 | tf_op jit(solution)/shard_map/reduce_scatter | solution.py:98
  998.0 18.3 all-to-all-start.5
  1025.9 241.0 %copy-start.8 = (f32[16,1,4,1,64,64]{4,5,3,2,1,0:T(8,128)S(1)}, f32[16,1,4,1,64,64]{4,5,3,2,1,0:T(8,128)}, u32[]{:S(2)}) copy-start(f32[16,1,4,1,64,64]{4,5,3,2,1,0:T(8,128)} %copy-done.7) | copy-start | bytes 3145732
  1290.5 17.7 all-to-all-start.7
  1308.2 20.7 all-to-all-start.8
  1328.9 21.0 all-to-all-start.6
  1333.2 321.2 %reduce-scatter.7.cloned.1.call-start = ((), (), s32[]{:S(2)}) async-start(), calls=%async_computation.18 | async-start | bytes 28311552 | tf_op jit(solution)/shard_map/reduce_scatter | solution.py:98
  1386.2 6.0 collective-permute-start.1
  1407.9 691.0 %reduce-scatter.13.cloned.1.call-start = ((), (), s32[]{:S(2)}) async-start(), calls=%async_computation.21 | async-start | bytes 51904512
  1430.7 799.0 %all-reduce.20.cloned.1.call-start = ((), (), s32[]{:S(2)}) async-start(), calls=%async_computation.22 | async-start | bytes 524288 | tf_op jit(solution)/shard_map/psum | solution.py:242
  1450.1 1028.9 %all-reduce.22.cloned.1.call-start = ((), (), s32[]{:S(2)}) async-start(), calls=%async_computation.23 | async-start | bytes 25690112 | tf_op jit(solution)/shard_map/psum | solution.py:104
  (83 other events, 987.1 us)
Sparse Core Ops, SparseCore 0:
  9.7 223.4 all-gather.6
  234.8 80.2 all-gather.8
  316.8 391.8 all-gather.10
  710.1 200.9 all-gather.12
  961.2 87.8 reduce-scatter.8
  1051.2 225.7 reduce-scatter.10
  1408.0 246.3 reduce-scatter.6
  1656.8 442.0 reduce-scatter.12
  2106.1 123.5 all-reduce.19
  2234.0 244.9 all-reduce.21
where the time goes:
time: 2520 us; the launch traced here: 2500 us
  waiting for transfers between devices  1260 us (50%)
  matrix products  546 us (22%)
  other arithmetic  419 us (17%)
  blocking collectives  119 us (5%)
  local copies, waits for them, and re-layouts  103 us (4%)
  starting transfers between devices  41.7 us (2%)
    unnamed x11, waiting for transfers between devices  447 us
    another operation x5, other arithmetic, delta_rule(): lax.linalg.triangular_solve(system, targets, left_side=True, lower=True,...  318 us
    psum x1, waiting for transfers between devices, reduce_rows(): return lax.psum(summed, 'seq').astype(jnp.float32)  247 us
    reduce_scatter x3, waiting for transfers between devices, reduce_rows(): lax.psum_scatter(term(jnp.int32(0), total_rows // shards * lax.axis_size(...  204 us
    all_gather x1, waiting for transfers between devices, per_device(): lax.all_gather(w_qkv, 'fsdp', axis=0, tiled=True)  153 us
    dot_general x48, matrix products, advance(): result = jnp.einsum('shcd,shde->shce', query_part, state, precision=HIGH)  92.6 us
    dot_general x48, matrix products, advance(): jnp.einsum('shcd,shce->shde', key_raw, fresh, precision=HIGH)  90 us
    all_gather x1, waiting for transfers between devices, per_device(): down_full = lax.all_gather(w_down, 'fsdp', axis=0, tiled=True)  83.8 us
  transfers between devices with their start and end apart: 21, of which 14 were waited for; matrix products, arithmetic and copies ran while one was open for 39% of the time, Pallas kernels for 0%

commit v1 on v0

--- a/solution.py
+++ b/solution.py
@@ -8,6 +8,24 @@
 SPAN = 64
 EPS = 1e-06
 HIGH = lax.Precision.HIGHEST
+
+
+def laid_out(parts, dim):
+    shape = list(parts.shape[1:])
+    shape[dim] *= parts.shape[0]
+    return jnp.moveaxis(parts, 0, dim).reshape(shape)
+
+
+def collected_by_bits(array, axis):
+    size = lax.axis_size(axis)
+    parts = array[None]
+    for level in range(size.bit_length() - 1):
+        bit = 1 << level
+        partner_block = lax.ppermute(parts, axis, [(i, i ^ bit) for i in range(size)])
+        both = jnp.stack([parts, partner_block])
+        upper = lax.axis_index(axis) >> level & 1
+        parts = jnp.where(upper == 0, both, both[::-1]).reshape(-1, *array.shape)
+    return parts
 
 
 def from_behind(array, axis, by):
@@ -133,7 +151,7 @@
         lax.all_gather(w_gate_up, "fsdp", axis=0, tiled=True),
     )
     gain_first, qkv_full, beta_full, conv_full, out_full, gain_second, gate_up_full = gathered
-    down_full = lax.all_gather(w_down, "fsdp", axis=0, tiled=True)
+    down_full = laid_out(collected_by_bits(w_down, "fsdp"), 0)
     sequences, block, width = inputs.shape
     tokens = sequences * block
     hidden_width = down_full.shape[0]

time: 2520 us -> 3550 us (1.41)
  blocking collectives: 119 us -> 1020 us
  other arithmetic: 419 us -> 494 us
  waiting for transfers between devices: 1260 us -> 1320 us
    all_gather x1, blocking collectives: 24.1 us -> 657 us  [per_device(): lax.all_gather(w_beta, 'fsdp', axis=0, tiled=True)]
    ppermute x0 -> x3, waiting for transfers between devices: none -> 327 us  [collected_by_bits(): lax.ppermute(parts, axis, [(i, i ^ bit) for i in range(size)])]
    all_gather x1, blocking collectives: 13.6 us -> 295 us  [per_device(): lax.all_gather(norm1_gain, 'fsdp', axis=0, tiled=True)]
    all_gather x1, waiting for transfers between devices: 153 us -> 0.02 us  [per_device(): lax.all_gather(w_qkv, 'fsdp', axis=0, tiled=True)]
    all_gather x1 -> x0, waiting for transfers between devices: 83.8 us -> none  [per_device(): down_full = lax.all_gather(w_down, 'fsdp', axis=0, tiled=True)]
    another operation x1 -> x5, other arithmetic: 0.01 us -> 36.6 us  [the longest x4 36.6 us: collected_by_bits(): both = jnp.stack([parts, partner_block])]
    unnamed x11 -> x10, waiting for transfers between devices: 447 us -> 447 us
  transfers between devices with their start and end apart: 21 -> 23, of which waited for: 14 -> 12; matrix products, arithmetic and copies ran while one was open for 39% -> 29% of each run, Pallas kernels for 0% -> 0%
where the time goes in v1:
time: 3550 us; the launch traced here: 3530 us
  waiting for transfers between devices  1320 us (37%)
  blocking collectives  1020 us (29%)
  matrix products  538 us (15%)
  other arithmetic  494 us (14%)
  local copies, waits for them, and re-layouts  94.4 us (3%)
  starting transfers between devices  46.5 us (1%)
    all_gather x1, blocking collectives, per_device(): lax.all_gather(w_beta, 'fsdp', axis=0, tiled=True)  657 us
    unnamed x10, waiting for transfers between devices  447 us
    ppermute x3, waiting for transfers between devices, collected_by_bits(): lax.ppermute(parts, axis, [(i, i ^ bit) for i in range(size)])  327 us
    another operation x5, other arithmetic, delta_rule(): lax.linalg.triangular_solve(system, targets, left_side=True, lower=True,...  318 us
    all_gather x1, blocking collectives, per_device(): lax.all_gather(norm1_gain, 'fsdp', axis=0, tiled=True)  295 us
    psum x1, waiting for transfers between devices, reduce_rows(): return lax.psum(summed, 'seq').astype(jnp.float32)  247 us
    reduce_scatter x3, waiting for transfers between devices, reduce_rows(): lax.psum_scatter(term(jnp.int32(0), total_rows // shards * lax.axis_size(...  204 us
    dot_general x48, matrix products, advance(): result = jnp.einsum('shcd,shde->shce', query_part, state, precision=HIGH)  82.6 us
  transfers between devices with their start and end apart: 23, of which 12 were waited for; matrix products, arithmetic and copies ran while one was open for 29% of the time, Pallas kernels for 0%

profile of v1, /device:TPU:0, one launch (start us, length us, event | category | flops | bytes accessed | tf_op | source)
XLA Modules:
  0.0 3531.5 jit_solution(115439523687575222)
XLA Ops:
  30.0 321.6 %collective-permute-done.2 = bf16[2,704,2048]{2,1,0:T(8,128)(2,1)} collective-permute-done((bf16[2,704,2048]{2,1,0:T(8,128)(2,1)}, bf16[2,704,2048]{2,1,0:T(8,128)(2,1)}, u32[]{:S(2)}, u32[]{:S(2)}) %collective-permute-start.2) | collective-permute-done | bytes 5767200 | tf_op jit(solution)/shard_map/ppermute | solution.py:24
  365.1 295.0 %all-gather = bf16[8,1,256]{2,1,0:T(2,128)(2,1)S(1)} all-gather(bf16[1,1,256]{2,1,0:T(2,128)(2,1)S(1)} %reshape.1120), channel_id=1, replica_groups=mesh['fsdp'=8,'seq'=4] {'fsdp'}, dimensions={0}, use_global_device_ids=true | all-gather | bytes 4608 | tf_op jit(solution)/shard_map/all_gather | solution.py:145
  660.1 656.8 %all_gather.24 = bf16[2048,16]{0,1:T(8,128)(2,1)S(1)} all-gather(bf16[256,16]{0,1:T(8,128)(2,1)S(1)} %copy-done.79), channel_id=1, replica_groups=mesh['fsdp'=8,'seq'=4] {'fsdp'}, dimensions={0}, use_global_device_ids=true | all-gather | bytes 73728 | tf_op jit(solution)/shard_map/all_gather | solution.py:147
  1323.8 13.9 all_gather.23
  1338.0 11.8 fusion.79
  1417.3 19.9 pad_maximum_fusion
  1445.0 315.2 %custom-call.7 = f32[16,1,4,1,64,64]{4,5,3,2,1,0:T(8,128)S(1)} custom-call(f32[16,1,4,1,64,64]{5,4,3,2,1,0:T(8,128)} %add_bitcast_fusion), custom_call_target="InvertDiagBlocksLowerTriangular" | custom-call | tf_op jit(solution)/shard_map/jvp()/triangular_solve | solution.py:84
  1776.4 97.0 %while.43 = (s32[]{:T(128)}, f32[1,4,128,128]{3,2,1,0:T(8,128)S(1)}, bf16[16,1,4,64,128]{4,3,0,2,1:T(8,128)(2,1)S(1)}, f32[16,1,4,128,128]{4,3,2,1,0:T(8,128)}, ...) while((s32[]{:T(128)}, ...), condition=%wide.region_3.4_spmd.clone, body=%wide.region_2.3_spmd.clone.sunk | while | flops 176553984 | bytes 3148948 | solution.py:100
  1879.9 28.2 reverse_select_fusion
  1926.7 24.9 fusion.212
  1951.6 28.3 multiply_convert_fusion.1
  1979.9 22.4 multiply_reduce_fusion.4
  2011.4 12.5 convolution_convert_fusion.1
  2051.7 13.0 all-to-all-done.5
  2072.9 230.3 %while.44 = (s32[]{:T(128)}, f32[1,4,128,128]{2,3,1,0:T(8,128)S(1)}, f32[16,1,4,64,128]{4,3,2,1,0:T(8,128)}, f32[16,1,4,64,128]{4,3,2,1,0:T(8,128)S(1)}, f32[16,...) while((s32[]{:T(128)}, ...), condition=%wide.region_9.10_spmd.clone, body=%wide.region_8.9_spmd.clone.sunk | while | flops 352747520 | bytes 4728510 | solution.py:100
  2424.3 14.0 convolution_convert_fusion.2
  2439.9 21.3 convolution_convert_fusion
  2480.3 203.5 %reduce-scatter.7.cloned.1.call-done = bf16[256,6144]{1,0:T(8,128)(2,1)} async-done(((bf16[2048,6144]{1,0:T(8,128)(2,1)}), bf16[256,6144]{1,0:T(8,128)(2,1)}) %reduce-scatter.7.cloned.1.call-update) | async-done | bytes 3145744 | tf_op jit(solution)/shard_map/reduce_scatter | solution.py:116
  2683.9 444.5 %reduce-scatter.13.cloned.1.call-done = bf16[256,11264]{1,0:T(8,128)(2,1)} async-done(((bf16[2048,11264]{1,0:T(8,128)(2,1)}), bf16[256,11264]{1,0:T(8,128)(2,1)}) %reduce-scatter.13.cloned.1.call-update) | async-done | bytes 5767184
  3129.1 12.4 fusion.107
  3143.3 14.5 fusion.112
  3157.7 38.2 %all-reduce.14 = (f32[2048]{0:T(1024)S(1)}, f32[128]{0:T(128)}, f32[2048]{0:T(1024)S(1)}) all-reduce(f32[2048]{0:T(1024)S(1)} %get-tuple-element.617, f32[128]{0:T(128)S(1)} %bitcast_reduce_fusion, f32[2048]{0:T(1024)S(1)} %copy-done.81), channel_id=1, replica_groups=mesh['fsdp'=8,'seq'=4] {'fsdp','seq'}, use_global_device_ids=true, to_apply=%region_16.17 | all-reduce | flops 4224 | bytes 33792 | tf_op jit(solution)/shard_map/psum | solution.py:260
  3200.6 58.5 %all-reduce.20.cloned.1.call-done = (f32[2048,16]{0,1:T(8,128)}, f32[2048,12]{0,1:T(8,128)}) async-done(((f32[2048,16]{0,1:T(8,128)}, f32[2048,12]{0,1:T(8,128)}), (f32[2048,16]{0,1:T(8,128)}, f32[2048,12]{0,1:T(8,128)})) %all-reduce.20.cloned.1.call-update) | async-done | bytes 229392 | tf_op jit(solution)/shard_map/psum | solution.py:260
  3261.8 246.8 %all-reduce.22.cloned.1.call-done = (bf16[256,6144]{1,0:T(8,128)(2,1)}, bf16[256,2048]{1,0:T(8,128)(2,1)}, bf16[256,11264]{1,0:T(8,128)(2,1)}, bf16[704,2048]{1,0:T(8,128)(2,1)}) async-done(((bf16[256,6144]{1,0:T(8,128)(2,1)}, bf16[256,2048]{1,0:T(8,128)(2,1)}, bf16[256,11264]{1,0:T(8,128)(2,1)}, bf16[704,2048]{1,0:T(8,128)(2,1)}), (bf16[256,6144]{1,0:T(8,128)(2,1)}, bf16[256,2048]{1,0:T(8,128)(2,1)}, ...) | async-done | bytes 12845072 | tf_op jit(solution)/shard_map/psum | solution.py:122
  (599 shorter events, 697.7 us)
Async XLA Ops:
  7.2 1330.9 %all-gather.6.cloned.1.call-start = ((), (), s32[]{:S(2)}) async-start(), calls=%async_computation.14 | async-start | bytes 28311552 | tf_op jit(solution)/shard_map/all_gather | solution.py:146
  7.9 1911.3 %all-gather.8.cloned.1.call-start = ((), (), s32[]{:S(2)}) async-start(), calls=%async_computation.15 | async-start | bytes 9437184 | tf_op jit(solution)/shard_map/all_gather | solution.py:149
  8.7 1918.0 %all-gather.10.cloned.1.call-start = ((), (), s32[]{:S(2)}) async-start(), calls=%async_computation.16 | async-start | bytes 51904512 | tf_op jit(solution)/shard_map/all_gather | solution.py:151
  10.5 5.5 collective-permute-start.1
  26.8 324.8 %collective-permute-start.2 = (bf16[2,704,2048]{2,1,0:T(8,128)(2,1)}, bf16[2,704,2048]{2,1,0:T(8,128)(2,1)}, u32[]{:S(2)}, u32[]{:S(2)}) collective-permute-start(bf16[2,704,2048]{2,1,0:T(8,128)(2,1)} %get-tuple-element.694), channel_id=1, source_target_pairs={{0,8},{4,12},{8,0},{12,4},{16,24},{20,28},{24,16},{28,20},{1,9},{5... | collective-permute-start | bytes 17301512 | tf_op jit(solution)/shard_map/ppermute | solution.py:24
  357.5 959.4 %copy-start.26 = (bf16[1,256,2048]{2,1,0:T(8,128)(2,1)S(1)}, bf16[1,256,2048]{2,1,0:T(8,128)(2,1)}, u32[]{:S(2)}) copy-start(bf16[1,256,2048]{2,1,0:T(8,128)(2,1)} %param.17) | copy-start | bytes 3145732
  364.5 1052.8 %collective-permute-start.3 = (bf16[4,704,2048]{2,1,0:T(8,128)(2,1)}, bf16[4,704,2048]{2,1,0:T(8,128)(2,1)}, u32[]{:S(2)}, u32[]{:S(2)}) collective-permute-start(bf16[4,704,2048]{2,1,0:T(8,128)(2,1)} %bitcast.56), channel_id=1, source_target_pairs={{0,16},{4,20},{8,24},{12,28},{16,0},{20,4},{24,8},{28,12},{1,17},{... | collective-permute-start | bytes 34603016 | tf_op jit(solution)/shard_map/ppermute | solution.py:24
  1320.1 57.6 %all-to-all-start.1 = ((bf16[4,2,512]{2,1,0:T(2,128)(2,1)}), bf16[4,2,512]{2,1,0:T(2,128)(2,1)S(1)}, u32[]{:S(2)}, u32[]{:S(2)}) async-start(bf16[4,2,512]{2,1,0:T(2,128)(2,1)} %reshape.1141), calls=%async_computation.1 | async-start | bytes 16384 | tf_op jit(solution)/shard_map/all_to_all | solution.py:179
  1351.6 14.2 collective-permute-start
  1377.8 18.1 all-to-all-start.2
  1395.9 17.9 all-to-all-start.3
  1413.8 27.4 all-to-all-start
  1875.2 32.9 all-to-all-start.4
  1879.5 600.9 %reduce-scatter.9.cloned.1.call-start = ((), (), s32[]{:S(2)}) async-start(), calls=%async_computation.18 | async-start | bytes 9437184 | tf_op jit(solution)/shard_map/reduce_scatter | solution.py:116
  2011.3 469.0 %reduce-scatter.11.cloned.1.call-start = ((), (), s32[]{:S(2)}) async-start(), calls=%async_computation.19 | async-start | bytes 25952256 | tf_op jit(solution)/shard_map/reduce_scatter | solution.py:116
  2047.2 17.5 all-to-all-start.5
  2308.8 30.1 all-to-all-start.8
  2338.9 17.8 all-to-all-start.7
  2356.7 16.6 all-to-all-start.6
  2360.2 323.7 %reduce-scatter.7.cloned.1.call-start = ((), (), s32[]{:S(2)}) async-start(), calls=%async_computation.17 | async-start | bytes 28311552 | tf_op jit(solution)/shard_map/reduce_scatter | solution.py:116
  2416.9 6.0 collective-permute-start.4
  2438.3 690.1 %reduce-scatter.13.cloned.1.call-start = ((), (), s32[]{:S(2)}) async-start(), calls=%async_computation.20 | async-start | bytes 51904512
  2461.2 798.0 %all-reduce.20.cloned.1.call-start = ((), (), s32[]{:S(2)}) async-start(), calls=%async_computation.21 | async-start | bytes 524288 | tf_op jit(solution)/shard_map/psum | solution.py:260
  2480.0 1028.6 %all-reduce.22.cloned.1.call-start = ((), (), s32[]{:S(2)}) async-start(), calls=%async_computation.22 | async-start | bytes 25690112 | tf_op jit(solution)/shard_map/psum | solution.py:122
  (90 other events, 4472.2 us)
Sparse Core Ops, SparseCore 0:
  9.7 339.8 all-gather.5
  351.2 366.5 all-gather.7
  719.4 577.0 all-gather.9
  2011.4 88.2 reduce-scatter.8
  2101.9 225.7 reduce-scatter.10
  2438.4 245.3 reduce-scatter.6
  2686.3 442.0 reduce-scatter.12
  3135.6 123.5 all-reduce.19
  3263.6 244.9 all-reduce.21
